TPU v7x, 32 devices: a whole 2x2x4 slice. The times are simulated.
32 devices in a mesh: grp: 2 (over y), seq: 4 (over z), dp: 2 (over x), pipe: 2 (over core).
Axes of the slice: x: 2, y: 2, z: 4, core: 2. Of those that a mesh axis runs over, the one named last changes fastest.
Arguments:
- embeddings: bfloat16 [4, 512, 1664], P(('grp', 'dp'), 'seq'), parts along dimension 0, may hold values from -650 to 650
- upstream: bfloat16 [4, 512, 1664], P(('grp', 'dp'), 'seq'), parts along dimension 0, may hold values from -6 to 6
- attn_weights: bfloat16 [4, 1664, 832], P(None, ('seq', 'dp'), 'pipe'), may hold values from -1.2747549 to 1.2747549
Outputs:
- input_grads: bfloat16 [4, 512, 1664], P(('grp', 'dp'), 'seq'), parts along dimension 0
- weight_grads: float32 [8, 1664, 832], P('grp', ('seq', 'dp'), 'pipe'), parts along dimension 0
There are 2 independent parts, one for each index of `grp`. A program takes and returns all parts, laid end to end along the dimension named above; an argument that names none is the same for every part. Nothing has to cross between parts.
All inputs are finite; a program needn't handle non-finite values.
Results may differ from a plain program's by a relative error of at most 0.014.
The roundings to bfloat16 on the way count: a program that leaves them out, or rounds other values in their place, can miss the bound.
Values may be sent and summed in bfloat16 or wider, within the bound.
No kernel may reach another device: no remote copies, remote signals or barrier semaphores. Data moves between devices by JAX's collectives and lax.ppermute only.
A program may use at most 128 MiB of HBM per device.

v0:
```python
import math
import jax
import jax.numpy as jnp
from jax import lax
from jax.sharding import PartitionSpec as P

HD = 104
EPSILON = 1e-06


def local(embeddings, upstream, attn_weights):
    tokens = embeddings[0]
    row_gradients = upstream[0]
    row_count = tokens.shape[0]
    weights = lax.all_gather(attn_weights, ("seq", "dp"), axis=1, tiled=True)
    local_width = weights.shape[2]
    head_count = local_width // HD
    score_scale = HD ** (-0.5)
    features = tokens.astype(jnp.float32)
    row_mean = jnp.mean(features, axis=1, keepdims=True)
    mean_removed = features - row_mean
    variance = jnp.mean(mean_removed * mean_removed, axis=1, keepdims=True)
    inverse_deviation = lax.rsqrt(variance + EPSILON)
    standardized_input = mean_removed * inverse_deviation
    normalized_rows = standardized_input.astype(jnp.bfloat16)
    proj = jnp.einsum(
        "td,cdh->cth", normalized_rows, weights[:3], preferred_element_type=jnp.float32
    ).astype(jnp.bfloat16)
    gathered = lax.all_gather(proj[1:], "seq", axis=1, tiled=True)
    key_count = gathered.shape[1]
    query_heads = proj[0].reshape(row_count, head_count, HD).transpose(1, 0, 2)
    key_heads = gathered[0].reshape(key_count, head_count, HD).transpose(1, 0, 2)
    value_heads = gathered[1].reshape(key_count, head_count, HD).transpose(1, 0, 2)
    grad_att = jnp.dot(row_gradients, weights[3], preferred_element_type=jnp.float32).astype(
        jnp.bfloat16
    )
    grad_heads = grad_att.reshape(row_count, head_count, HD).transpose(1, 0, 2)

    def one_head(items):
        query_rows, key_rows, value_rows, grad_out = items
        scores = jnp.dot(query_rows, key_rows.T, preferred_element_type=jnp.float32) * score_scale
        row_max = jnp.max(scores, axis=1, keepdims=True)
        log_total = row_max + jnp.log(jnp.sum(jnp.exp(scores - row_max), axis=1, keepdims=True))
        probs = jnp.exp(scores - log_total).astype(jnp.bfloat16)
        attended = jnp.dot(probs, value_rows, preferred_element_type=jnp.float32).astype(
            jnp.bfloat16
        )
        row_delta = jnp.sum(
            grad_out.astype(jnp.float32) * attended.astype(jnp.float32), axis=1, keepdims=True
        )
        dprobs = jnp.dot(grad_out, value_rows.T, preferred_element_type=jnp.float32)
        dscores = (probs.astype(jnp.float32) * (dprobs - row_delta) * score_scale).astype(
            jnp.bfloat16
        )
        grad_q = jnp.dot(dscores, key_rows, preferred_element_type=jnp.float32).astype(jnp.bfloat16)
        key_term = jnp.dot(dscores.T, query_rows, preferred_element_type=jnp.float32)
        value_term = jnp.dot(probs.T, grad_out, preferred_element_type=jnp.float32)
        return (attended, grad_q, key_term, value_term)

    attended_h, grad_q_h, key_h, value_h = lax.map(
        one_head, (query_heads, key_heads, value_heads, grad_heads)
    )
    attended_flat = attended_h.transpose(1, 0, 2).reshape(row_count, local_width)
    grad_q = grad_q_h.transpose(1, 0, 2).reshape(1, row_count, local_width)
    key_terms = key_h.transpose(1, 0, 2).reshape(key_count, local_width)
    value_terms = value_h.transpose(1, 0, 2).reshape(key_count, local_width)
    both_terms = jnp.stack([key_terms, value_terms])
    owned = lax.psum_scatter(
        both_terms.astype(jnp.bfloat16), "seq", scatter_dimension=1, tiled=True
    )
    grad_qkv = jnp.concatenate([grad_q, owned], axis=0)
    token_count = row_count * lax.axis_size("seq") * lax.axis_size("dp")
    grad_factor = 1.0 / math.sqrt(token_count)
    terms_qkv = jnp.einsum(
        "td,cth->cdh", normalized_rows, grad_qkv, preferred_element_type=jnp.float32
    )
    term_out = jnp.einsum(
        "td,th->dh", row_gradients, attended_flat, preferred_element_type=jnp.float32
    )
    terms = jnp.concatenate([terms_qkv, term_out[None]], axis=0) * grad_factor
    seq_summed = lax.psum_scatter(
        terms.astype(jnp.bfloat16), "seq", scatter_dimension=1, tiled=True
    )
    weight_grads = lax.psum_scatter(seq_summed, "dp", scatter_dimension=1, tiled=True).astype(
        jnp.float32
    )
    input_part = jnp.einsum(
        "cth,cdh->td", grad_qkv, weights[:3], preferred_element_type=jnp.float32
    )
    reduced_total = lax.psum(input_part.astype(jnp.bfloat16), "pipe").astype(jnp.float32)
    leading_term = jnp.mean(reduced_total, axis=1, keepdims=True)
    trailing_term = jnp.mean(reduced_total * standardized_input, axis=1, keepdims=True)
    input_gradient = (
        row_gradients.astype(jnp.float32)
        + inverse_deviation * (reduced_total - leading_term - standardized_input * trailing_term)
    ).astype(jnp.bfloat16)
    return (input_gradient[None], weight_grads)


def solution(mesh):
    in_specs = (
        P(("grp", "dp"), "seq", None),
        P(("grp", "dp"), "seq", None),
        P(None, ("seq", "dp"), "pipe"),
    )
    out_specs = (P(("grp", "dp"), "seq", None), P("grp", ("seq", "dp"), "pipe"))
    return jax.shard_map(local, mesh=mesh, in_specs=in_specs, out_specs=out_specs, check_vma=False)
```

profile of v0, /device:TPU:0, one launch (start us, length us, event | category | flops | bytes accessed | tf_op | source)
XLA Modules:
  0.0 409.7 jit_solution(12918442514962170128)
XLA Ops:
  7.2 2.7 copy.16
  10.0 1.1 convert_reduce_fusion.1
  11.2 1.3 fusion.46
  12.5 106.6 %all-gather.2.cloned.1.call-done = bf16[4,1664,416]{2,0,1:T(4,128)(2,1)} async-done(((bf16[4,208,416]{2,0,1:T(4,128)(2,1)}), bf16[4,1664,416]{2,0,1:T(4,128)(2,1)}) %all-gather.2.cloned.1.call-update) | async-done | bytes 5537808 | tf_op jit(solution)/shard_map/all_gather | solution.py:15
  119.0 11.3 %copy.29 = bf16[3,1664,416]{1,2,0:T(8,128)(2,1)} copy(bf16[3,1664,416]{2,0,1:T(4,128)(2,1)} %bitcast.176) | data formatting | bytes 8306688
  130.3 3.5 fusion.33
  134.5 8.4 %slice.30 = bf16[1,1664,416]{2,0,1:T(2,128)(2,1)} slice(bf16[4,1664,416]{2,0,1:T(4,128)(2,1)} %all-gather.2.cloned.1.call-done), slice={[3:4], [0:1664], [0:416]} | slice | bytes 2768896 | tf_op jit(solution)/shard_map/slice | solution.py:34
  142.9 8.5 %copy.30 = bf16[1,1664,416]{1,2,0:T(8,128)(2,1)S(1)} copy(bf16[1,1664,416]{2,0,1:T(2,128)(2,1)} %slice.30) | data formatting | bytes 2768896
  151.5 18.4 %all_gather.7 = bf16[2,512,416]{1,2,0:T(8,128)(2,1)S(1)} all-gather(bf16[2,128,416]{1,2,0:T(8,128)(2,1)} %slice.27), channel_id=1, replica_groups=mesh['grp'=2,'seq'=4,'dp'=2,'pipe'=2] {'seq'}, dimensions={1}, use_global_device_ids=true | all-gather | bytes 1064960 | tf_op jit(solution)/shard_map/all_gather | solution.py:29
  169.9 1.0 fusion.57
  170.9 1.3 copy.19
  172.2 1.3 copy.20
  174.0 16.9 %while.16 = (s32[]{:T(128)}, bf16[4,128,104]{1,2,0:T(8,128)(2,1)}, bf16[4,128,104]{1,2,0:T(8,128)(2,1)}, bf16[4,512,104]{1,2,0:T(8,128)(2,1)}, bf16[4,512,104]{1...) while((s32[]{:T(128)}, bf16[4,128,104]{1,2,0:T(8,128)(2,1)}, ...), condition=%wide.region_6.7_spmd, body=%wide.region_2.6_spmd.sunk | while | flops 82589440 | bytes 2916977 | solution.py:60
  191.0 1.2 pad_maximum_fusion
  192.2 1.0 copy.23
  193.2 1.7 reshape.49
  195.0 1.5 convolution_bitcast_fusion.3
  196.5 21.9 %reduce-scatter.10.cloned.1.call-done = bf16[128,832]{1,0:T(8,128)(2,1)} async-done(((bf16[512,832]{1,0:T(8,128)(2,1)}), bf16[128,832]{1,0:T(8,128)(2,1)}) %reduce-scatter.10.cloned.1.call-update) | async-done | bytes 213008
  218.5 1.9 reshape.50
  220.4 1.1 copy.24
  221.5 1.3 convolution_bitcast_fusion.2
  222.9 3.3 fusion.29
  226.1 11.9 %copy.25 = bf16[4,1664,416]{2,0,1:T(4,128)(2,1)} copy(bf16[4,1664,416]{1,2,0:T(8,128)(2,1)} %fusion.29) | data formatting | bytes 11075584
  238.1 12.9 %reshape.51 = bf16[1664,1664]{1,0:T(8,128)(2,1)} reshape(bf16[1664,4,416]{2,1,0:T(4,128)(2,1)} %bitcast.175) | data formatting | bytes 11075584
  251.0 3.8 fusion.30
  255.1 93.5 %reduce-scatter.12.cloned.1.call-done = bf16[416,1664]{1,0:T(8,128)(2,1)} async-done(((bf16[1664,1664]{1,0:T(8,128)(2,1)}), bf16[416,1664]{1,0:T(8,128)(2,1)}) %reduce-scatter.12.cloned.1.call-update) | async-done | bytes 1384464
  348.6 21.9 %all-reduce.2.cloned.1.call-done = bf16[128,1664]{1,0:T(8,128)(2,1)} async-done(((bf16[128,1664]{1,0:T(8,128)(2,1)}), bf16[128,1664]{1,0:T(8,128)(2,1)}) %all-reduce.2.cloned.1.call-update) | async-done | bytes 426000 | tf_op jit(solution)/shard_map/psum | solution.py:90
  370.5 1.3 convert_reduce_fusion
  371.8 2.2 fusion.48
  374.0 23.8 %reduce-scatter.14.cloned.1.call-done = bf16[208,1664]{1,0:T(8,128)(2,1)} async-done(((bf16[416,1664]{1,0:T(8,128)(2,1)}), bf16[208,1664]{1,0:T(8,128)(2,1)}) %reduce-scatter.14.cloned.1.call-update) | async-done | bytes 692240
  397.8 3.1 reshape.54
  401.7 1.5 copy.22
  (72 shorter events, 19.5 us)
Async XLA Ops:
  7.2 111.9 %all-gather.2.cloned.1.call-start = ((), (), s32[]{:S(2)}) async-start(), calls=%async_computation.3 | async-start | bytes 7667712 | tf_op jit(solution)/shard_map/all_gather | solution.py:15
  10.0 208.5 %reduce-scatter.10.cloned.1.call-start = ((), (), s32[]{:S(2)}) async-start(), calls=%async_computation.5 | async-start | bytes 1146880
  119.0 11.3 %copy-start = (bf16[1,128,1664]{2,1,0:T(8,128)(2,1)S(1)}, bf16[1,128,1664]{2,1,0:T(8,128)(2,1)}, u32[]{:S(2)}) copy-start(bf16[1,128,1664]{2,1,0:T(8,128)(2,1)} %param.5) | copy-start | bytes 1277956
  142.9 30.6 %copy-start.1 = (bf16[1,128,1664]{2,1,0:T(8,128)(2,1)S(1)}, bf16[1,128,1664]{2,1,0:T(8,128)(2,1)}, u32[]{:S(2)}) copy-start(bf16[1,128,1664]{2,1,0:T(8,128)(2,1)} %param.6) | copy-start | bytes 1277956
  191.0 4.0 copy-start.4
  192.2 29.3 %copy-start.3 = (bf16[4,128,104]{1,2,0:T(8,128)(2,1)S(1)}, bf16[4,128,104]{1,2,0:T(8,128)(2,1)}, u32[]{:S(2)}) copy-start(bf16[4,128,104]{1,2,0:T(8,128)(2,1)} %get-tuple-element.52) | copy-start | bytes 319492
  195.0 153.6 %reduce-scatter.12.cloned.1.call-start = ((), (), s32[]{:S(2)}) async-start(), calls=%async_computation.6 | async-start | bytes 6922240
  251.0 120.9 %copy-start.2 = (bf16[1,128,1664]{2,1,0:T(8,128)(2,1)S(1)}, bf16[1,128,1664]{2,1,0:T(8,128)(2,1)}, u32[]{:S(2)}) copy-start(bf16[1,128,1664]{2,1,0:T(8,128)(2,1)} %param.6) | copy-start | bytes 1277956
  251.0 119.5 %all-reduce.2.cloned.1.call-start = ((), (), s32[]{:S(2)}) async-start(), calls=%async_computation.4 | async-start | bytes 851968 | tf_op jit(solution)/shard_map/psum | solution.py:90
  254.8 143.0 %reduce-scatter.14.cloned.1.call-start = ((), (), s32[]{:S(2)}) async-start(), calls=%async_computation.7 | async-start | bytes 2076672
Sparse Core Ops, SparseCore 0:
  10.8 108.2 all-gather.1
  195.1 23.3 reduce-scatter.9
  251.1 97.4 reduce-scatter.11
  351.4 19.0 all-reduce.1
  372.6 25.1 reduce-scatter.13
where the time goes:
time: 411 us; the launch traced here: 410 us
  waiting for transfers between devices  268 us (65%)
  local copies, waits for them, and re-layouts  71.1 us (17%)
  matrix products  26 us (6%)
  blocking collectives  18.4 us (4%)
  between operations  13.9 us (3%)
  other arithmetic  11.9 us (3%)
    unnamed x8, waiting for transfers between devices  139 us
    all_gather x1, waiting for transfers between devices, local(): weights = lax.all_gather(attn_weights, ('seq', 'dp'), axis=1, tiled=True)  107 us
    unnamed x22, local copies, waits for them, and re-layouts  58.4 us
    psum x1, waiting for transfers between devices, local(): lax.psum(input_part.astype(jnp.bfloat16), 'pipe').astype(jnp.float32)  21.9 us
    all_gather x1, blocking collectives, local(): gathered = lax.all_gather(proj[1:], 'seq', axis=1, tiled=True)  18.4 us
    slice x1, local copies, waits for them, and re-layouts, local(): weights[3]  8.39 us
  transfers between devices with their start and end apart: 5, of which 5 were waited for; matrix products, arithmetic and copies ran while one was open for 3% of the time, Pallas kernels for 0%

commit v1 on v0

--- a/solution.py
+++ b/solution.py
@@ -26,7 +26,17 @@
     proj = jnp.einsum(
         "td,cdh->cth", normalized_rows, weights[:3], preferred_element_type=jnp.float32
     ).astype(jnp.bfloat16)
-    gathered = lax.all_gather(proj[1:], "seq", axis=1, tiled=True)
+    x = proj[1:]
+    ways = lax.axis_size("seq")
+    up = [(d, (d + 1) % ways) for d in range(ways)]
+    down = [(d, (d - 1) % ways) for d in range(ways)]
+    earlier, later = ([x], [x])
+    for _ in range(ways // 2):
+        earlier.append(lax.ppermute(earlier[-1], "seq", up))
+    for _ in range((ways - 1) // 2):
+        later.append(lax.ppermute(later[-1], "seq", down))
+    line = jnp.concatenate([*earlier[::-1], *later[1:]], axis=1)
+    gathered = jnp.roll(line, (lax.axis_index("seq") - ways // 2) * x.shape[1], axis=1)
     key_count = gathered.shape[1]
     query_heads = proj[0].reshape(row_count, head_count, HD).transpose(1, 0, 2)
     key_heads = gathered[0].reshape(key_count, head_count, HD).transpose(1, 0, 2)

time: 411 us -> 394 us (0.959)
  blocking collectives: 18.4 us -> 0 us
  waiting for transfers between devices: 268 us -> 276 us
  matrix products: 26 us -> 18.7 us
    all_gather x1 -> x0, blocking collectives: 18.4 us -> none  [local(): gathered = lax.all_gather(proj[1:], 'seq', axis=1, tiled=True)]
    ppermute x0 -> x3, waiting for transfers between devices: none -> 7.27 us  [the longest x2 7.27 us: local(): earlier.append(lax.ppermute(earlier[-1], 'seq', up))]
    unnamed x22 -> x27, local copies, waits for them, and re-layouts: 58.4 us -> 59.2 us
  transfers between devices with their start and end apart: 5 -> 8, of which waited for: 5 -> 6; matrix products, arithmetic and copies ran while one was open for 3% -> 7% of each run, Pallas kernels for 0% -> 0%
where the time goes in v1:
time: 394 us; the launch traced here: 392 us
  waiting for transfers between devices  276 us (70%)
  local copies, waits for them, and re-layouts  69.1 us (18%)
  matrix products  18.7 us (5%)
  between operations  14 us (4%)
  other arithmetic  9.75 us (2%)
  starting transfers between devices  4.32 us (1%)
    unnamed x8, waiting for transfers between devices  138 us
    all_gather x1, waiting for transfers between devices, local(): weights = lax.all_gather(attn_weights, ('seq', 'dp'), axis=1, tiled=True)  109 us
    unnamed x27, local copies, waits for them, and re-layouts  59.2 us
    psum x1, waiting for transfers between devices, local(): lax.psum(input_part.astype(jnp.bfloat16), 'pipe').astype(jnp.float32)  21.9 us
    slice x1, local copies, waits for them, and re-layouts, local(): weights[3]  8.39 us
  transfers between devices with their start and end apart: 8, of which 6 were waited for; matrix products, arithmetic and copies ran while one was open for 7% of the time, Pallas kernels for 0%

profile of v1, /device:TPU:0, one launch (start us, length us, event | category | flops | bytes accessed | tf_op | source)
XLA Modules:
  0.0 392.1 jit_solution(6043234576132205269)
XLA Ops:
  7.2 2.8 copy.16
  10.5 108.6 %all-gather.2.cloned.1.call-done = bf16[4,1664,416]{2,0,1:T(4,128)(2,1)} async-done(((bf16[4,208,416]{2,0,1:T(4,128)(2,1)}), bf16[4,1664,416]{2,0,1:T(4,128)(2,1)}) %all-gather.2.cloned.1.call-update) | async-done | bytes 5537808 | tf_op jit(solution)/shard_map/all_gather | solution.py:15
  119.1 11.2 %copy.29 = bf16[3,1664,416]{1,2,0:T(8,128)(2,1)} copy(bf16[3,1664,416]{2,0,1:T(4,128)(2,1)} %bitcast.176) | data formatting | bytes 8306688
  130.3 3.5 fusion.33
  134.5 3.9 collective-permute-start.2
  138.4 8.4 %slice.28 = bf16[1,1664,416]{2,0,1:T(2,128)(2,1)} slice(bf16[4,1664,416]{2,0,1:T(4,128)(2,1)} %all-gather.2.cloned.1.call-done), slice={[3:4], [0:1664], [0:416]} | slice | bytes 2768896 | tf_op jit(solution)/shard_map/slice | solution.py:44
  146.7 8.5 %copy.30 = bf16[1,1664,416]{1,2,0:T(8,128)(2,1)S(1)} copy(bf16[1,1664,416]{2,0,1:T(2,128)(2,1)} %slice.28) | data formatting | bytes 2768896
  156.0 7.3 %collective-permute-done.1 = bf16[2,128,416]{1,2,0:T(8,128)(2,1)S(1)} collective-permute-done((bf16[2,128,416]{1,2,0:T(8,128)(2,1)S(1)}, bf16[2,128,416]{1,2,0:T(8,128)(2,1)S(1)}, u32[]{:S(2)}, u32[]{:S(2)}) %collective-permute-start.1) | collective-permute-done | bytes 213024 | tf_op jit(solution)/shard_map/ppermute | solution.py:35
  164.9 9.7 %while.16 = (s32[]{:T(128)}, bf16[4,128,104]{1,2,0:T(8,128)(2,1)S(1)}, bf16[4,128,104]{1,2,0:T(8,128)(2,1)S(1)}, bf16[4,512,104]{1,2,0:T(8,128)(2,1)}, bf16[4,51...) while((s32[]{:T(128)}, ...), condition=%wide.region_6.7_spmd, body=%wide.region_2.6_spmd.sunk | while | flops 82589440 | bytes 2916977 | solution.py:70
  166.2 0.9 fusion.90
  168.7 0.9 fusion.90
  171.1 0.9 fusion.90
  173.5 0.9 fusion.90
  174.6 1.1 pad_maximum_fusion
  175.7 1.0 copy.23
  176.6 1.7 reshape.49
  178.4 1.5 convolution_bitcast_fusion.3
  180.0 20.9 %reduce-scatter.10.cloned.1.call-done = bf16[128,832]{1,0:T(8,128)(2,1)} async-done(((bf16[512,832]{1,0:T(8,128)(2,1)}), bf16[128,832]{1,0:T(8,128)(2,1)}) %reduce-scatter.10.cloned.1.call-update) | async-done | bytes 213008
  200.9 1.9 reshape.50
  202.8 1.1 copy.24
  203.9 1.3 convolution_bitcast_fusion.2
  205.2 3.3 fusion.29
  208.5 11.9 %copy.25 = bf16[4,1664,416]{2,0,1:T(4,128)(2,1)} copy(bf16[4,1664,416]{1,2,0:T(8,128)(2,1)} %fusion.29) | data formatting | bytes 11075584
  220.4 12.9 %reshape.51 = bf16[1664,1664]{1,0:T(8,128)(2,1)} reshape(bf16[1664,4,416]{2,1,0:T(4,128)(2,1)} %bitcast.175) | data formatting | bytes 11075584
  233.6 3.7 fusion.30
  237.4 93.6 %reduce-scatter.12.cloned.1.call-done = bf16[416,1664]{1,0:T(8,128)(2,1)} async-done(((bf16[1664,1664]{1,0:T(8,128)(2,1)}), bf16[416,1664]{1,0:T(8,128)(2,1)}) %reduce-scatter.12.cloned.1.call-update) | async-done | bytes 1384464
  331.0 21.9 %all-reduce.2.cloned.1.call-done = bf16[128,1664]{1,0:T(8,128)(2,1)} async-done(((bf16[128,1664]{1,0:T(8,128)(2,1)}), bf16[128,1664]{1,0:T(8,128)(2,1)}) %all-reduce.2.cloned.1.call-update) | async-done | bytes 426000 | tf_op jit(solution)/shard_map/psum | solution.py:100
  352.9 1.3 convert_reduce_fusion
  354.2 2.2 fusion.48
  356.4 23.8 %reduce-scatter.14.cloned.1.call-done = bf16[208,1664]{1,0:T(8,128)(2,1)} async-done(((bf16[416,1664]{1,0:T(8,128)(2,1)}), bf16[208,1664]{1,0:T(8,128)(2,1)}) %reduce-scatter.14.cloned.1.call-update) | async-done | bytes 692240
  380.2 3.1 reshape.54
  384.1 1.5 copy.22
  (83 shorter events, 10.7 us)
Async XLA Ops:
  7.2 2.9 copy-start
  7.2 111.9 %all-gather.2.cloned.1.call-start = ((), (), s32[]{:S(2)}) async-start(), calls=%async_computation.3 | async-start | bytes 7667712 | tf_op jit(solution)/shard_map/all_gather | solution.py:15
  10.0 190.9 %reduce-scatter.10.cloned.1.call-start = ((), (), s32[]{:S(2)}) async-start(), calls=%async_computation.5 | async-start | bytes 1146880
  134.5 20.9 %collective-permute-start = (bf16[2,128,416]{1,2,0:T(8,128)(2,1)}, bf16[2,128,416]{1,2,0:T(8,128)(2,1)S(1)}, u32[]{:S(2)}, u32[]{:S(2)}) collective-permute-start(bf16[2,128,416]{1,2,0:T(8,128)(2,1)} %slice.27), channel_id=1, source_target_pairs={{0,4},{4,8},{8,12},{12,0},{1,5},{5,9},{9,13},{13,1},{2,6},{6,10},{... | collective-permute-start | bytes 638984 | tf_op jit(solution)/shard_map/ppermute | solution.py:35
  134.5 29.0 %collective-permute-start.2 = (bf16[2,128,416]{1,2,0:T(8,128)(2,1)}, bf16[2,128,416]{1,2,0:T(8,128)(2,1)S(1)}, u32[]{:S(2)}, u32[]{:S(2)}) collective-permute-start(bf16[2,128,416]{1,2,0:T(8,128)(2,1)} %slice.27), channel_id=1, source_target_pairs={{0,12},{4,0},{8,4},{12,8},{1,13},{5,1},{9,5},{13,9},{2,14},{6,2},{... | collective-permute-start | bytes 638984 | tf_op jit(solution)/shard_map/ppermute | solution.py:37
  146.7 8.7 %copy-start.1 = (bf16[1,128,1664]{2,1,0:T(8,128)(2,1)S(1)}, bf16[1,128,1664]{2,1,0:T(8,128)(2,1)}, u32[]{:S(2)}) copy-start(bf16[1,128,1664]{2,1,0:T(8,128)(2,1)} %param.6) | copy-start | bytes 1277956
  155.4 7.9 %collective-permute-start.1 = (bf16[2,128,416]{1,2,0:T(8,128)(2,1)S(1)}, bf16[2,128,416]{1,2,0:T(8,128)(2,1)S(1)}, u32[]{:S(2)}, u32[]{:S(2)}) collective-permute-start(bf16[2,128,416]{1,2,0:T(8,128)(2,1)S(1)} %collective-permute-done), channel_id=1, source_target_pairs={{0,4},{4,8},{8,12},{12,0},{1,5},{5,9},{9,13},{13,1},{2,6},{6,10},{... | collective-permute-start | bytes 638984 | tf_op jit(solution)/shard_map/ppermute | solution.py:35
  163.9 1.0 copy-start.3
  178.4 152.6 %reduce-scatter.12.cloned.1.call-start = ((), (), s32[]{:S(2)}) async-start(), calls=%async_computation.6 | async-start | bytes 6922240
  233.4 119.5 %all-reduce.2.cloned.1.call-start = ((), (), s32[]{:S(2)}) async-start(), calls=%async_computation.4 | async-start | bytes 851968 | tf_op jit(solution)/shard_map/psum | solution.py:100
  237.3 116.9 %copy-start.2 = (bf16[1,128,1664]{2,1,0:T(8,128)(2,1)S(1)}, bf16[1,128,1664]{2,1,0:T(8,128)(2,1)}, u32[]{:S(2)}) copy-start(bf16[1,128,1664]{2,1,0:T(8,128)(2,1)} %param.6) | copy-start | bytes 1277956
  237.3 142.8 %reduce-scatter.14.cloned.1.call-start = ((), (), s32[]{:S(2)}) async-start(), calls=%async_computation.7 | async-start | bytes 2076672
Sparse Core Ops, SparseCore 0:
  10.8 108.2 all-gather.1
  178.5 22.3 reduce-scatter.9
  233.5 97.4 reduce-scatter.11
  333.7 19.0 all-reduce.1
  355.0 25.1 reduce-scatter.13
